TPU v7x, 32 devices: a whole 2x2x4 slice. The times are simulated.
32 devices in a mesh: ctx: 8 (over z, y), head: 4 (over x, core).
Axes of the slice: x: 2, y: 2, z: 4, core: 2. Of those that a mesh axis runs over, the one named last changes fastest.
Arguments:
- signal: bfloat16 [4096, 4096], P('ctx', 'head'), may hold values from -6 to 6
- gate_input: bfloat16 [4096, 4096], P('ctx', 'head'), may hold values from -6 to 6
- input_map: bfloat16 [4096, 1024], P('ctx', 'head'), may hold values from -0.5 to 0.5
- readout: bfloat16 [4096, 1024], P('ctx', 'head'), may hold values from -0.5 to 0.5
- log_decay: float32 [64, 4096], P('head', 'ctx'), may hold values from -1.3 to 0
- skip_gain: float32 [64], P('head'), may hold values from 0.5 to 1.5
- norm_gain: float32 [4096], P('head'), may hold values from 0.5 to 1.5
- out_weight: bfloat16 [4096, 2048], P('head'), may hold values from -0.09375 to 0.09375
- out_grad: bfloat16 [4096, 2048], P(('ctx', 'head')), may hold values from -8 to 8
Outputs:
- layer_out: bfloat16 [4096, 2048], P(('ctx', 'head'))
- signal_grad: float32 [4096, 4096], P('ctx', 'head')
- gate_grad: float32 [4096, 4096], P('ctx', 'head')
- input_map_grad: float32 [4096, 1024], P('ctx', 'head')
- readout_grad: float32 [4096, 1024], P('ctx', 'head')
- decay_grad: float32 [64, 4096], P('head', 'ctx')
- skip_grad: float32 [64], P('head')
- gain_grad: float32 [4096], P('head')
- weight_grad: float32 [4096, 2048], P('head')
All inputs are finite; a program needn't handle non-finite values.
Results may differ from a plain program's by a relative error of at most 0.0049.
Values may be sent and summed in bfloat16 or wider, within the bound.
A program may use at most 128 MiB of HBM per device.

v0:
```python
from functools import partial

import jax
import jax.numpy as jnp
from jax import lax
from jax.experimental import pallas as pl
from jax.experimental.pallas import tpu as pltpu
from jax.sharding import PartitionSpec as P

P_SIZE = 64
N = 128
CHUNK = 256
F32 = jnp.float32
BF16 = jnp.bfloat16
VMEM_LIMIT = 52 * 1024 * 1024

NN = (((1,), (0,)), ((), ()))
NT = (((1,), (1,)), ((), ()))
TN = (((0,), (0,)), ((), ()))


def mm(a, b, dims=NN):
    return lax.dot_general(a, b, dims, preferred_element_type=F32)


def spread(factor, width):
    rows = factor.shape[0]
    left = lax.broadcasted_iota(jnp.int32, (rows, 128), 1) < P_SIZE
    pairs = []
    for k in range(width // 128):
        a = jnp.broadcast_to(factor[:, 2 * k : 2 * k + 1], (rows, 128))
        b = jnp.broadcast_to(factor[:, 2 * k + 1 : 2 * k + 2], (rows, 128))
        pairs.append(jnp.where(left, a, b))
    return jnp.concatenate(pairs, axis=1)


def cumulated(log_row):
    heads, length = log_row.shape
    hi = log_row.astype(BF16).astype(F32)
    rest = log_row - hi
    mid = rest.astype(BF16).astype(F32)
    low = rest - mid
    parts = jnp.concatenate([hi, mid, low, jnp.zeros_like(hi)], axis=0).astype(BF16)
    upper = (
        lax.broadcasted_iota(jnp.int32, (length, length), 0)
        <= lax.broadcasted_iota(jnp.int32, (length, length), 1)
    )
    sums = mm(parts, jnp.where(upper, 1.0, 0.0).astype(BF16))
    row = sums[0:heads] + sums[heads : 2 * heads] + sums[2 * heads : 3 * heads]
    col = jnp.transpose(jnp.concatenate([row] * (128 // heads), axis=0))
    return row, col


def decays(col, width):
    heads = width // P_SIZE
    col = col[:, :heads]
    from_start = jnp.exp(col)
    to_closing = jnp.exp(col[-1:, :] - col)
    return spread(from_start, width), spread(to_closing, width)


def chunks_of(total):
    return [(c, slice(c * CHUNK, (c + 1) * CHUNK)) for c in range(total // CHUNK)]


def in_parts(values):
    width = values[0].shape[1]
    at = lax.broadcasted_iota(jnp.int32, (8, width), 0)
    rows = jnp.zeros((8, width), F32)
    for i, value in enumerate(values):
        hi = value.astype(BF16).astype(F32)
        mid = (value - hi).astype(BF16).astype(F32)
        for j, part in enumerate((hi, mid, value - hi - mid)):
            rows = jnp.where(at == 3 * i + j, part, rows)
    return rows.astype(BF16)


def local_state_kernel(x_ref, b_ref, log_ref, state_ref, decay_ref):
    tokens, width = x_ref.shape
    state = jnp.zeros((N, width), F32)
    decay = jnp.ones((1, width), F32)
    for _, at in chunks_of(tokens):
        _, col = cumulated(log_ref[:, at])
        from_start, to_closing = decays(col, width)
        span = from_start[-1:, :]
        scaled = (x_ref[at, :].astype(F32) * to_closing).astype(BF16)
        state = state * span + mm(b_ref[at, :], scaled, TN)
        decay = decay * span
    state_ref[0] = state.astype(BF16)
    decay_ref[0] = in_parts([decay])


def forward_kernel(
    x_ref, z_ref, b_ref, c_ref, log_ref, skip_ref, gain_ref, incoming_ref, rows_ref,
    core_ref, entry_ref, normed_ref, weight_ref,
):
    tokens, width = x_ref.shape
    state = incoming_ref[0].astype(F32)
    left = lax.broadcasted_iota(jnp.int32, (CHUNK, 128), 1) < P_SIZE
    lower = (
        lax.broadcasted_iota(jnp.int32, (CHUNK, CHUNK), 0)
        >= lax.broadcasted_iota(jnp.int32, (CHUNK, CHUNK), 1)
    )
    last = tokens // CHUNK - 1
    for c, at in chunks_of(tokens):
        row, col = cumulated(log_ref[:, at])
        from_start, to_closing = decays(col, width)
        x = x_ref[at, :]
        xf = x.astype(F32)
        bm, cm = b_ref[at, :], c_ref[at, :]
        inner = mm(cm, bm, NT)
        entry = state.astype(BF16)
        entry_ref[0, c] = entry
        pieces = []
        for k in range(width // 128):
            pair = x[:, 128 * k : 128 * k + 128]
            halves = []
            for h in (2 * k, 2 * k + 1):
                gap = jnp.where(lower, col[:, h : h + 1] - row[h : h + 1, :], -1e30)
                halves.append(mm((jnp.exp(gap) * inner).astype(BF16), pair))
            pieces.append(jnp.where(left, halves[0], halves[1]))
        core = jnp.concatenate(pieces, axis=1) + from_start * mm(cm, entry)
        core_ref[at, :] = core
        y = core + skip_ref[...] * xf
        z = z_ref[at, :].astype(F32)
        gated = y * (z * jax.nn.sigmoid(z))
        inv = lax.rsqrt(jnp.mean(gated * gated, axis=1, keepdims=True) + 1e-05)
        normed_ref[at, :] = (gated * inv * gain_ref[...]).astype(BF16)
        if c < last:
            scaled = (xf * to_closing).astype(BF16)
            state = state * from_start[-1:, :] + mm(bm, scaled, TN)
    columns = rows_ref.shape[1]
    tile = 512
    for n in range(columns // tile):
        cut = slice(n * tile, (n + 1) * tile)
        weight_ref[:, cut] = mm(normed_ref[...], rows_ref[:, cut], TN).astype(BF16)


def middle_kernel(
    x_ref, z_ref, c_ref, log_ref, skip_ref, gain_ref, core_ref, normed_ref, w_ref, rows_ref,
    layer_ref, dy_ref, gate_ref, later_ref, part_ref, total,
):
    tokens, width = x_ref.shape
    group = pl.program_id(0)
    groups = pl.num_programs(0)
    outflow = jnp.zeros((N, width), F32)
    gain_sum = jnp.zeros((1, width), F32)
    skip_sum = jnp.zeros((1, width), F32)
    gain = gain_ref[...]
    for _, at in reversed(chunks_of(tokens)):
        _, col = cumulated(log_ref[:, at])
        from_start = spread(jnp.exp(col[:, : width // P_SIZE]), width)
        dn = mm(rows_ref[at, :], w_ref[...], NT).astype(BF16).astype(F32)
        xf = x_ref[at, :].astype(F32)
        z = z_ref[at, :].astype(F32)
        y = core_ref[at, :] + skip_ref[...] * xf
        s = jax.nn.sigmoid(z)
        silu = z * s
        gated = y * silu
        inv = lax.rsqrt(jnp.mean(gated * gated, axis=1, keepdims=True) + 1e-05)
        gain_sum += jnp.sum(dn * gated * inv, axis=0, keepdims=True)
        scaled = gain * dn
        mean = jnp.mean(scaled * gated, axis=1, keepdims=True)
        dgated = inv * scaled - gated * (inv * inv * inv * mean)
        gate_ref[at, :] = dgated * y * s * (1.0 + z * (1.0 - s))
        dy = dgated * silu
        dy_ref[at, :] = dy
        skip_sum += jnp.sum(dy * xf, axis=0, keepdims=True)
        outflow = outflow * from_start[-1:, :] + mm(
            c_ref[at, :], (dy * from_start).astype(BF16), TN
        )
    later_ref[0] = outflow.astype(BF16)
    part_ref[0] = in_parts([gain_sum, skip_sum])
    columns = w_ref.shape[1]
    tile = 512
    for n in range(columns // tile):
        cut = slice(n * tile, (n + 1) * tile)
        piece = mm(normed_ref[...], w_ref[:, cut])

        @pl.when(group == 0)
        def _():
            total[:, cut] = piece

        @pl.when(group > 0)
        def _():
            total[:, cut] += piece

    @pl.when(group == groups - 1)
    def _():
        layer_ref[...] = total[...].astype(BF16)


def backward_kernel(
    x_ref, dy_ref, core_ref, b_ref, c_ref, log_ref, skip_ref, entry_ref, later_ref,
    signal_ref, map_ref, read_ref, decay_ref,
):
    tokens, width = x_ref.shape
    heads = width // P_SIZE
    outflow = later_ref[0].astype(F32)
    left = lax.broadcasted_iota(jnp.int32, (CHUNK, 128), 1) < P_SIZE
    upper = (
        lax.broadcasted_iota(jnp.int32, (CHUNK, CHUNK), 0)
        <= lax.broadcasted_iota(jnp.int32, (CHUNK, CHUNK), 1)
    )
    own = (
        lax.broadcasted_iota(jnp.int32, (heads, width), 1) // P_SIZE
        == lax.broadcasted_iota(jnp.int32, (heads, width), 0)
    )
    own = jnp.where(own, 1.0, 0.0).astype(BF16)
    for c, at in reversed(chunks_of(tokens)):
        row, col = cumulated(log_ref[:, at])
        from_start, to_closing = decays(col, width)
        x = x_ref[at, :]
        xf = x.astype(F32)
        dyf = dy_ref[at, :]
        dy = dyf.astype(BF16)
        bm, cm = b_ref[at, :], c_ref[at, :]
        inner = mm(bm, cm, NT)
        out = outflow.astype(BF16)
        pair_sum = jnp.zeros((CHUNK, CHUNK), F32)
        pieces = []
        for k in range(width // 128):
            cut = slice(128 * k, 128 * k + 128)
            x_pair, dy_pair = x[:, cut], dy[:, cut]
            halves = []
            for h, side in ((2 * k, left), (2 * k + 1, ~left)):
                gap = jnp.where(upper, row[h : h + 1, :] - col[:, h : h + 1], -1e30)
                fade = jnp.exp(gap)
                halves.append(mm((fade * inner).astype(BF16), dy_pair))
                one = jnp.where(side, xf[:, cut], 0.0).astype(BF16)
                pair_sum += mm(one, dy_pair, NT) * fade
            pieces.append(jnp.where(left, halves[0], halves[1]))
        core_grad = jnp.concatenate(pieces, axis=1) + to_closing * mm(bm, out)
        signal_ref[at, :] = core_grad + skip_ref[...] * dyf
        pair_sum = pair_sum.astype(BF16)
        map_ref[at, :] = mm(pair_sum, cm) + mm((xf * to_closing).astype(BF16), out, NT)
        dy_start = (dyf * from_start).astype(BF16)
        read_ref[at, :] = mm(pair_sum, bm, TN) + mm(dy_start, entry_ref[0, c], NT)
        slope = dyf * core_ref[at, :] - xf * core_grad
        hi = slope.astype(BF16)
        low = (slope - hi.astype(F32)).astype(BF16)
        decay_ref[:, at] = mm(own, hi, NT) + mm(own, low, NT)
        if c > 0:
            outflow = outflow * from_start[-1:, :] + mm(cm, dy_start, TN)


def params():
    return pltpu.CompilerParams(
        dimension_semantics=("arbitrary",), vmem_limit_bytes=VMEM_LIMIT
    )


def cost(flops, moved, exps=0):
    return pl.CostEstimate(flops=int(flops), bytes_accessed=int(moved), transcendentals=int(exps))


def entering(state, extra, reverse, fades=None):
    devices = lax.axis_size("ctx")
    groups, depth, width = state.shape
    share = depth // devices
    shares = state.reshape(groups, devices, share, width).transpose(1, 0, 2, 3)
    copies = jnp.broadcast_to(extra[None], (devices,) + extra.shape)
    sent = jnp.concatenate([shares, copies], axis=2)
    every = lax.all_to_all(sent, "ctx", split_axis=0, concat_axis=0, tiled=True)
    extras = every[:, :, share:].astype(F32)
    if fades is None:
        fades = jnp.sum(extras[:, :, 0:3], axis=2, keepdims=True)
    carried = jnp.zeros((groups, share, width), F32)
    found = [None] * devices
    for d in reversed(range(devices)) if reverse else range(devices):
        found[d] = carried.astype(BF16)
        carried = fades[d] * carried + every[d, :, :share].astype(F32)
    back = lax.all_to_all(jnp.stack(found), "ctx", split_axis=0, concat_axis=0, tiled=True)
    return back.transpose(1, 0, 2, 3).reshape(groups, depth, width), extras, fades


def summed(part, axis):
    devices = lax.axis_size(axis)
    rows, columns = part.shape
    terms = lax.all_to_all(part, axis, split_axis=0, concat_axis=0, tiled=True)
    terms = terms.reshape(devices, rows // devices, columns)
    return jnp.sum(terms.astype(F32), axis=0).astype(BF16)


def on_device(
    signal, gate_input, input_map, readout, log_decay, skip_gain, norm_gain, out_weight, out_grad
):
    tokens, features = signal.shape
    heads = log_decay.shape[0]
    groups = input_map.shape[1] // N
    in_group = heads // groups
    width = in_group * P_SIZE
    model = out_weight.shape[1]
    spans = tokens // CHUNK
    sds = jax.ShapeDtypeStruct
    wide = pl.BlockSpec((tokens, width), lambda g: (0, g))
    narrow = pl.BlockSpec((tokens, N), lambda g: (0, g))
    logs = pl.BlockSpec((in_group, tokens), lambda g: (g, 0))
    lane = pl.BlockSpec((1, width), lambda g: (0, g))
    state = pl.BlockSpec((1, N, width), lambda g: (g, 0, 0))
    fade = pl.BlockSpec((1, 8, width), lambda g: (g, 0, 0))
    entries = pl.BlockSpec((1, spans, N, width), lambda g: (g, 0, 0, 0))
    weight = pl.BlockSpec((width, model), lambda g: (g, 0))
    rows = pl.BlockSpec((tokens, model), lambda g: (0, 0))

    skip = jnp.repeat(skip_gain, P_SIZE).reshape(1, features)
    gain = norm_gain.reshape(1, features)
    piece = lax.all_gather(out_grad, "head", axis=0, tiled=True)

    own_state, own_fade = pl.pallas_call(
        local_state_kernel,
        grid=(groups,),
        in_specs=[wide, narrow, logs],
        out_specs=[state, fade],
        out_shape=[sds((groups, N, width), BF16), sds((groups, 8, width), BF16)],
        compiler_params=params(),
        cost_estimate=cost(2 * tokens * N * features, 3 * tokens * features),
        name="local_state",
    )(signal, input_map, log_decay)
    incoming, _, fades = entering(own_state, own_fade, False)

    core, entry, normed, weight_part = pl.pallas_call(
        forward_kernel,
        grid=(groups,),
        in_specs=[wide, wide, narrow, narrow, logs, lane, lane, state, rows],
        out_specs=[wide, entries, wide, weight],
        out_shape=[
            sds((tokens, features), F32),
            sds((groups, spans, N, width), BF16),
            sds((tokens, features), BF16),
            sds((features, model), BF16),
        ],
        compiler_params=params(),
        cost_estimate=cost(2 * tokens * features * model, 12 * tokens * features),
        name="forward",
    )(signal, gate_input, input_map, readout, log_decay, skip, gain, incoming, piece)
    weight_share = summed(weight_part, "ctx")
    weight_grad = lax.all_gather(weight_share, "ctx", axis=0, tiled=True).astype(F32)

    layer_part, dy, gate_grad, own_later, parts = pl.pallas_call(
        middle_kernel,
        grid=(groups,),
        in_specs=[wide, wide, narrow, logs, lane, lane, wide, wide, weight, rows],
        out_specs=[rows, wide, wide, state, fade],
        out_shape=[
            sds((tokens, model), BF16),
            sds((tokens, features), F32),
            sds((tokens, features), F32),
            sds((groups, N, width), BF16),
            sds((groups, 8, width), BF16),
        ],
        scratch_shapes=[pltpu.VMEM((tokens, model), F32)],
        compiler_params=params(),
        cost_estimate=cost(4 * tokens * features * model, 20 * tokens * features),
        name="middle",
    )(signal, gate_input, readout, log_decay, skip, gain, core, normed, out_weight, piece)
    layer_out = summed(layer_part, "head")
    later, parts, _ = entering(own_later, parts, True, fades)

    signal_grad, map_grad, read_grad, decay_grad = pl.pallas_call(
        backward_kernel,
        grid=(groups,),
        in_specs=[wide, wide, wide, narrow, narrow, logs, lane, entries, state],
        out_specs=[wide, narrow, narrow, logs],
        out_shape=[
            sds((tokens, features), F32),
            sds((tokens, groups * N), F32),
            sds((tokens, groups * N), F32),
            sds((heads, tokens), F32),
        ],
        compiler_params=params(),
        cost_estimate=cost(4 * tokens * features * model, 16 * tokens * features),
        name="backward",
    )(signal, dy, core, input_map, readout, log_decay, skip, entry, later)

    gain_grad = jnp.sum(parts[:, :, 0:3], axis=(0, 2)).reshape(features)
    skip_grad = jnp.sum(
        parts[:, :, 3:6].reshape(-1, groups, 3, in_group, P_SIZE), axis=(0, 2, 4)
    ).reshape(heads)
    return (
        layer_out,
        signal_grad,
        gate_grad,
        map_grad,
        read_grad,
        decay_grad,
        skip_grad,
        gain_grad,
        weight_grad,
    )


def solution(mesh):
    return jax.shard_map(
        on_device,
        mesh=mesh,
        in_specs=(
            P("ctx", "head"),
            P("ctx", "head"),
            P("ctx", "head"),
            P("ctx", "head"),
            P("head", "ctx"),
            P("head"),
            P("head"),
            P("head", None),
            P(("ctx", "head"), None),
        ),
        out_specs=(
            P(("ctx", "head"), None),
            P("ctx", "head"),
            P("ctx", "head"),
            P("ctx", "head"),
            P("ctx", "head"),
            P("head", "ctx"),
            P("head"),
            P("head"),
            P("head", None),
        ),
        check_vma=False,
    )
```

profile of v0, /device:TPU:0, one launch (start us, length us, event | category | flops | bytes accessed | tf_op | source)
XLA Modules:
  0.0 262.6 jit_solution(18019675604852032445)
XLA Ops:
  7.2 0.0 copy-start
  7.2 1.2 copy-done
  8.4 0.0 copy-start.2
  8.4 0.9 copy-done.2
  9.4 0.0 copy-start.4
  9.4 0.8 copy-done.4
  10.1 3.1 %local_state.1 = (bf16[2,128,512]{2,1,0:T(8,128)(2,1)S(1)}, bf16[2,8,512]{2,1,0:T(8,128)(2,1)S(1)}) custom-call(bf16[512,1024]{1,0:T(8,128)(2,1)S(1)} %copy-done, bf16[512,256]{1,0:T(8,128)(2,1)S(1)} %copy-done.2, f32[16,512]{1,0:T(8,128)S(1)} %copy-done.4), custom_call_target="tpu_custom_call" | custom-call | flops 134217728 | bytes 1572864 | tf_op jit(solution)/shard_map/local_state/pallas_call | solution.py:310
  13.3 0.0 copy-start.9
  13.3 0.8 pad_maximum_fusion
  14.1 0.0 copy-start.3
  14.1 0.0 copy-start.5
  14.1 0.0 copy-start.6
  14.1 0.0 copy-start.7
  14.1 7.4 %all-to-all-start = ((bf16[8,2,24,512]{3,2,1,0:T(8,128)(2,1)}), bf16[8,2,24,512]{3,2,1,0:T(8,128)(2,1)S(1)}, u32[]{:S(2)}, u32[]{:S(2)}) async-start(bf16[8,2,24,512]{3,2,1,0:T(8,128)(2,1)} %pad_maximum_fusion), calls=%async_computation | async-start | bytes 786432 | tf_op jit(solution)/shard_map/all_to_all | solution.py:264
  21.5 0.0 all-gather.3.cloned.1.call-start
  21.6 0.7 all-gather.3.cloned.1.call-update
  22.3 0.6 constant_dynamic-update-slice_fusion.7
  22.9 10.3 %all-to-all-done = bf16[8,2,24,512]{3,2,1,0:T(8,128)(2,1)S(1)} async-done(((bf16[8,2,24,512]{3,2,1,0:T(8,128)(2,1)}), bf16[8,2,24,512]{3,2,1,0:T(8,128)(2,1)S(1)}, u32[]{:S(2)}, u32[]{:S(2)}) %all-to-all-start) | async-done | bytes 393248 | tf_op jit(solution)/shard_map/all_to_all | solution.py:264
  33.4 0.6 constant_dynamic-update-slice_fusion.6
  34.0 0.6 constant_dynamic-update-slice_fusion.5
  34.6 0.6 constant_dynamic-update-slice_fusion.4
  35.3 0.6 constant_dynamic-update-slice_fusion.3
  35.9 0.7 constant_dynamic-update-slice_fusion.2
  36.6 0.6 constant_dynamic-update-slice_fusion.1
  37.2 0.6 constant_dynamic-update-slice_fusion
  37.8 3.6 %all-to-all-start.1 = ((bf16[8,2,16,512]{3,2,1,0:T(8,128)(2,1)}), bf16[8,2,16,512]{3,2,1,0:T(8,128)(2,1)S(1)}, u32[]{:S(2)}, u32[]{:S(2)}) async-start(bf16[8,2,16,512]{3,2,1,0:T(8,128)(2,1)} %constant_dynamic-update-slice_fusion), calls=%async_computation.1 | async-start | bytes 524288 | tf_op jit(solution)/shard_map/all_to_all | solution.py:273
  41.4 0.0 all-gather.5.cloned.1.call-start
  41.5 0.0 copy-done.9
  41.5 0.1 broadcast_in_dim.6
  41.6 0.1 reshape_reshape.3.skip_ref
  41.6 8.6 %all-to-all-done.1 = bf16[8,2,16,512]{3,2,1,0:T(8,128)(2,1)S(1)} async-done(((bf16[8,2,16,512]{3,2,1,0:T(8,128)(2,1)}), bf16[8,2,16,512]{3,2,1,0:T(8,128)(2,1)S(1)}, u32[]{:S(2)}, u32[]{:S(2)}) %all-to-all-start.1) | async-done | bytes 262176 | tf_op jit(solution)/shard_map/all_to_all | solution.py:273
  50.2 0.0 all-gather.3.cloned.1.call-done.rows_ref
  50.3 0.0 copy-done.3
  50.3 0.0 copy-done.5
  50.3 0.0 copy-done.6
  50.3 0.0 copy-done.7
  50.3 11.2 %forward.1 = (f32[512,1024]{1,0:T(8,128)}, bf16[2,2,128,512]{3,2,1,0:T(8,128)(2,1)S(1)}, bf16[512,1024]{1,0:T(8,128)(2,1)}, bf16[1024,2048]{1,0:T(8,128)(2,1)}) custom-call(bf16[512,1024]{1,0:T(8,128)(2,1)} %x_ref.7, bf16[512,1024]{1,0:T(8,128)(2,1)} %z_ref.3, bf16[512,256]{1,0:T(8,128)(2,1)S(1)} %copy-done.3, bf16[512,256]{1,0:T(8,128)(2,1)S(1)} %copy-done.6, ...), custom_call_target="tpu_custom_call" | custom-call | flops 2147483648 | bytes 6291456 | tf_op jit(solution)/shard_map/forward/pallas_call | solution.py:322
  61.5 97.1 %all_to_all.38 = bf16[8,128,2048]{2,1,0:T(8,128)(2,1)} all-to-all(bf16[8,128,2048]{2,1,0:T(8,128)(2,1)} %bitcast.41), channel_id=1, replica_groups=mesh['ctx'=8,'head'=4] {'ctx'}, dimensions={0} | all-to-all | bytes 8388608 | tf_op jit(solution)/shard_map/all_to_all | solution.py:280
  158.6 0.0 copy-start.1
  158.6 3.9 %reduce_sum.64 = bf16[128,2048]{1,0:T(8,128)(2,1)} reduce(bf16[8,128,2048]{2,1,0:T(8,128)(2,1)} %all_to_all.38, bf16[]{:T(256)} %constant.2.clone.1), dimensions={0}, to_apply=%region_5.6 | reduce | flops 1835008 | bytes 4718594 | tf_op jit(solution)/shard_map/reduce_sum | solution.py:282
  162.5 0.0 all-gather.5.cloned.1.call-update
  162.6 0.0 copy-done.1
  162.6 14.6 %middle.1 = (bf16[512,2048]{1,0:T(8,128)(2,1)}, f32[512,1024]{1,0:T(8,128)}, f32[512,1024]{1,0:T(8,128)}, bf16[2,128,512]{2,1,0:T(8,128)(2,1)S(1)}, bf16[2,8,512]{2,1,0:T(8,128)(2,1)S(1)}) custom-call(bf16[512,1024]{1,0:T(8,128)(2,1)S(1)} %copy-done.1, bf16[512,1024]{1,0:T(8,128)(2,1)} %z_ref.3, bf16[512,256]{1,0:T(8,128)(2,1)S(1)} %copy-done.6, ...), custom_call_target="tpu_custom_call" | custom-call | flops 4294967296 | bytes 10485760 | tf_op jit(solution)/shard_map/middle/pallas_call | solution.py:340
  177.2 0.8 pad_maximum_fusion.1
  178.0 3.5 %all-to-all-start.3 = ((bf16[8,2,24,512]{3,2,1,0:T(8,128)(2,1)}), bf16[8,2,24,512]{3,2,1,0:T(8,128)(2,1)S(1)}, u32[]{:S(2)}, u32[]{:S(2)}) async-start(bf16[8,2,24,512]{3,2,1,0:T(8,128)(2,1)} %pad_maximum_fusion.1), calls=%async_computation.3 | async-start | bytes 786432 | tf_op jit(solution)/shard_map/all_to_all | solution.py:264
  181.4 17.2 %all-to-all-done.3 = bf16[8,2,24,512]{3,2,1,0:T(8,128)(2,1)S(1)} async-done(((bf16[8,2,24,512]{3,2,1,0:T(8,128)(2,1)}), bf16[8,2,24,512]{3,2,1,0:T(8,128)(2,1)S(1)}, u32[]{:S(2)}, u32[]{:S(2)}) %all-to-all-start.3) | async-done | bytes 393248 | tf_op jit(solution)/shard_map/all_to_all | solution.py:264
  198.6 0.0 copy-start.8
  198.6 0.1 constant_dynamic-update-slice_fusion.15
  198.8 19.7 %all_to_all.39 = bf16[8,2,16,512]{3,2,1,0:T(8,128)(2,1)S(1)} all-to-all(bf16[8,2,16,512]{3,2,1,0:T(8,128)(2,1)S(1)} %constant_dynamic-update-slice_fusion.8), channel_id=1, replica_groups=mesh['ctx'=8,'head'=4] {'ctx'}, dimensions={0} | all-to-all | bytes 524288 | tf_op jit(solution)/shard_map/all_to_all | solution.py:273
  218.5 0.0 copy-done.8
  218.5 3.6 %all-to-all-start.2 = ((bf16[4,128,2048]{2,1,0:T(8,128)(2,1)}), bf16[4,128,2048]{2,1,0:T(8,128)(2,1)S(1)}, u32[]{:S(2)}, u32[]{:S(2)}) async-start(bf16[4,128,2048]{2,1,0:T(8,128)(2,1)} %bitcast.42), calls=%async_computation.2 | async-start | bytes 4194304 | tf_op jit(solution)/shard_map/all_to_all | solution.py:280
  222.1 0.9 slice_convert_fusion
  223.1 0.1 slice_reduce_fusion
  223.1 0.6 copy.52
  223.7 0.1 reduce_sum.61
  223.8 0.1 reduce_sum.62
  223.9 0.6 reshape.84
  224.5 10.7 %backward.1 = (f32[512,1024]{1,0:T(8,128)}, f32[512,256]{1,0:T(8,128)}, f32[512,256]{1,0:T(8,128)}, f32[16,512]{1,0:T(8,128)}) custom-call(bf16[512,1024]{1,0:T(8,128)(2,1)} %x_ref.7, f32[512,1024]{1,0:T(8,128)} %get-tuple-element.29.dy_ref, f32[512,1024]{1,0:T(8,128)} %get-tuple-element.26.core_ref, bf16[512,256]{1,0:T(8,128)(2,1)S(1)} %copy-done.3, ...), custom_call_target="tpu_custom_call" | custom-call | flops 4294967296 | bytes 8388608 | tf_op jit(solution)/shard_map/backward/pallas_call | solution.py:360
  235.2 12.6 %all-to-all-done.2 = bf16[4,128,2048]{2,1,0:T(8,128)(2,1)S(1)} async-done(((bf16[4,128,2048]{2,1,0:T(8,128)(2,1)}), bf16[4,128,2048]{2,1,0:T(8,128)(2,1)S(1)}, u32[]{:S(2)}, u32[]{:S(2)}) %all-to-all-start.2) | async-done | bytes 2097184 | tf_op jit(solution)/shard_map/all_to_all | solution.py:280
  247.8 1.3 reduce_sum.59
  249.1 0.0 all-gather.5.cloned.1.call-done
  249.1 6.7 %convert_element_type.194 = f32[1024,2048]{1,0:T(8,128)} convert(bf16[1024,2048]{1,0:T(8,128)(2,1)} %all-gather.5.cloned.1.call-done) | non-fusion elementwise | flops 2097152 | bytes 12582912 | tf_op jit(solution)/shard_map/convert_element_type | solution.py:338
  (21 shorter events, 0.3 us)
Async XLA Ops:
  7.2 1.2 copy-start
  8.4 0.9 copy-start.2
  9.4 0.8 copy-start.4
  13.3 28.2 %copy-start.9 = (f32[16]{0:T(128)S(1)}, f32[16]{0:T(128)}, u32[]{:S(2)}) copy-start(f32[16]{0:T(128)} %param.14) | copy-start | bytes 196
  14.1 36.2 %copy-start.3 = (bf16[512,256]{1,0:T(8,128)(2,1)S(1)}, bf16[512,256]{1,0:T(8,128)(2,1)}, u32[]{:S(2)}) copy-start(bf16[512,256]{1,0:T(8,128)(2,1)} %b_ref.5) | copy-start | bytes 786436
  14.1 36.2 %copy-start.5 = (f32[16,512]{1,0:T(8,128)S(1)}, f32[16,512]{1,0:T(8,128)}, u32[]{:S(2)}) copy-start(f32[16,512]{1,0:T(8,128)} %log_ref.7) | copy-start | bytes 98308
  14.1 36.2 %copy-start.6 = (bf16[512,256]{1,0:T(8,128)(2,1)S(1)}, bf16[512,256]{1,0:T(8,128)(2,1)}, u32[]{:S(2)}) copy-start(bf16[512,256]{1,0:T(8,128)(2,1)} %c_ref.5) | copy-start | bytes 786436
  14.1 36.2 %copy-start.7 = (f32[1024]{0:T(1024)S(1)}, f32[1024]{0:T(1024)}, u32[]{:S(2)}) copy-start(f32[1024]{0:T(1024)} %param.15) | copy-start | bytes 12292
  14.1 19.1 %all-to-all-start = ((bf16[8,2,24,512]{3,2,1,0:T(8,128)(2,1)}), bf16[8,2,24,512]{3,2,1,0:T(8,128)(2,1)S(1)}, u32[]{:S(2)}, u32[]{:S(2)}) async-start(bf16[8,2,24,512]{3,2,1,0:T(8,128)(2,1)} %pad_maximum_fusion), calls=%async_computation | async-start | bytes 786432 | tf_op jit(solution)/shard_map/all_to_all | solution.py:264
  21.5 28.7 %all-gather.3.cloned.1.call-start = ((), (), s32[]{:S(2)}) async-start(), calls=%async_computation.6 | async-start | bytes 2621440 | tf_op jit(solution)/shard_map/all_gather | solution.py:308
  37.8 12.4 %all-to-all-start.1 = ((bf16[8,2,16,512]{3,2,1,0:T(8,128)(2,1)}), bf16[8,2,16,512]{3,2,1,0:T(8,128)(2,1)S(1)}, u32[]{:S(2)}, u32[]{:S(2)}) async-start(bf16[8,2,16,512]{3,2,1,0:T(8,128)(2,1)} %constant_dynamic-update-slice_fusion), calls=%async_computation.1 | async-start | bytes 524288 | tf_op jit(solution)/shard_map/all_to_all | solution.py:273
  41.4 207.7 %all-gather.5.cloned.1.call-start = ((), (), s32[]{:S(2)}) async-start(), calls=%async_computation.7 | async-start | bytes 4718592 | tf_op jit(solution)/shard_map/all_gather | solution.py:338
  158.6 4.0 %copy-start.1 = (bf16[512,1024]{1,0:T(8,128)(2,1)S(1)}, bf16[512,1024]{1,0:T(8,128)(2,1)}, u32[]{:S(2)}) copy-start(bf16[512,1024]{1,0:T(8,128)(2,1)} %x_ref.7) | copy-start | bytes 3145732
  178.0 20.6 %all-to-all-start.3 = ((bf16[8,2,24,512]{3,2,1,0:T(8,128)(2,1)}), bf16[8,2,24,512]{3,2,1,0:T(8,128)(2,1)S(1)}, u32[]{:S(2)}, u32[]{:S(2)}) async-start(bf16[8,2,24,512]{3,2,1,0:T(8,128)(2,1)} %pad_maximum_fusion.1), calls=%async_computation.3 | async-start | bytes 786432 | tf_op jit(solution)/shard_map/all_to_all | solution.py:264
  198.6 19.9 %copy-start.8 = (bf16[8,2,24,512]{3,2,1,0:T(8,128)(2,1)}, bf16[8,2,24,512]{3,2,1,0:T(8,128)(2,1)S(1)}, u32[]{:S(2)}) copy-start(bf16[8,2,24,512]{3,2,1,0:T(8,128)(2,1)S(1)} %all-to-all-done.3) | copy-start | bytes 1179652
  218.5 29.3 %all-to-all-start.2 = ((bf16[4,128,2048]{2,1,0:T(8,128)(2,1)}), bf16[4,128,2048]{2,1,0:T(8,128)(2,1)S(1)}, u32[]{:S(2)}, u32[]{:S(2)}) async-start(bf16[4,128,2048]{2,1,0:T(8,128)(2,1)} %bitcast.42), calls=%async_computation.2 | async-start | bytes 4194304 | tf_op jit(solution)/shard_map/all_to_all | solution.py:280
Sparse Core Ops, SparseCore 0:
  23.9 23.9 all-gather.2
  162.7 82.4 all-gather.4
where the time goes:
time: 263 us
  blocking collectives  117 us (44%)
  waiting for transfers between devices  49.4 us (19%)
  Pallas kernels  39.6 us (15%)
  other arithmetic  19.2 us (7%)
  starting transfers between devices  18.2 us (7%)
  between operations  14.3 us (5%)
  local copies, waits for them, and re-layouts  5.14 us (2%)
    all_to_all x1, blocking collectives, summed(): terms = lax.all_to_all(part, axis, split_axis=0, concat_axis=0, tiled=True)  97.1 us
    all_to_all x2, waiting for transfers between devices, entering(): every = lax.all_to_all(sent, 'ctx', split_axis=0, concat_axis=0, tiled=True)  27.5 us
    all_to_all x1, blocking collectives, entering(): lax.all_to_all(jnp.stack(found), 'ctx', split_axis=0, concat_axis=0, tile...  19.7 us
    pallas_call x1, Pallas kernels, on_device(): pl.pallas_call(middle_kernel, grid=(groups,), in_specs=[wide, wide, narro...  14.6 us
    all_to_all x1, waiting for transfers between devices, summed(): terms = lax.all_to_all(part, axis, split_axis=0, concat_axis=0, tiled=True)  12.6 us
    pallas_call x1, Pallas kernels, on_device(): pl.pallas_call(forward_kernel, grid=(groups,), in_specs=[wide, wide, narr...  11.2 us
    all_to_all x2, starting transfers between devices, entering(): every = lax.all_to_all(sent, 'ctx', split_axis=0, concat_axis=0, tiled=True)  10.9 us
    pallas_call x1, Pallas kernels, on_device(): pl.pallas_call(backward_kernel, grid=(groups,), in_specs=[wide, wide, wid...  10.7 us
  transfers between devices with their start and end apart: 6, of which 4 were waited for; matrix products, arithmetic and copies ran while one was open for 4% of the time, Pallas kernels for 10%

commit v1 on v0

--- a/solution.py
+++ b/solution.py
@@ -334,8 +334,12 @@
         cost_estimate=cost(2 * tokens * features * model, 12 * tokens * features),
         name="forward",
     )(signal, gate_input, input_map, readout, log_decay, skip, gain, incoming, piece)
-    weight_share = summed(weight_part, "ctx")
-    weight_grad = lax.all_gather(weight_share, "ctx", axis=0, tiled=True).astype(F32)
+    half = features // 2
+    weight_halves = []
+    for at in (slice(0, half), slice(half, features)):
+        weight_share = summed(weight_part[at], "ctx")
+        weight_halves.append(lax.all_gather(weight_share, "ctx", axis=0, tiled=True))
+    weight_grad = jnp.concatenate([part.astype(F32) for part in weight_halves], axis=0)
 
     layer_part, dy, gate_grad, own_later, parts = pl.pallas_call(
         middle_kernel,

time: 263 us -> 264 us (level)
  blocking collectives: 117 us -> 67.1 us
  waiting for transfers between devices: 49.4 us -> 89.3 us
  starting transfers between devices: 18.2 us -> 23.7 us
  local copies, waits for them, and re-layouts: 5.14 us -> 9.21 us
    all_to_all x1 -> x2, waiting for transfers between devices: 12.6 us -> 63.1 us  [summed(): terms = lax.all_to_all(part, axis, split_axis=0, concat_axis=0, tiled=True)]
    all_to_all x1, blocking collectives: 97.1 us -> 51.7 us  [summed(): terms = lax.all_to_all(part, axis, split_axis=0, concat_axis=0, tiled=True)]
    all_to_all x2, waiting for transfers between devices: 27.5 us -> 16.5 us  [entering(): every = lax.all_to_all(sent, 'ctx', split_axis=0, concat_axis=0, tiled=True)]
    convert_element_type x1 -> x0, other arithmetic: 6.65 us -> none  [on_device(): lax.all_gather(weight_share, 'ctx', axis=0, tiled=True).astype(F32)]
    concatenate x0 -> x1, other arithmetic: none -> 6.52 us  [on_device(): jnp.concatenate([part.astype(F32) for part in weight_halves], axis=0)]
    all_to_all x1 -> x2, starting transfers between devices: 3.61 us -> 8.89 us  [summed(): terms = lax.all_to_all(part, axis, split_axis=0, concat_axis=0, tiled=True)]
    all_to_all x1, blocking collectives: 19.7 us -> 15.4 us  [entering(): lax.all_to_all(jnp.stack(found), 'ctx', split_axis=0, concat_axis=0, tile...]
    slice x0 -> x1, local copies, waits for them, and re-layouts: none -> 4.08 us  [on_device(): weight_share = summed(weight_part[at], 'ctx')]
  transfers between devices with their start and end apart: 6 -> 8, of which waited for: 4 -> 6; matrix products, arithmetic and copies ran while one was open for 4% -> 6% of each run, Pallas kernels for 10% -> 10%
where the time goes in v1:
time: 264 us
  waiting for transfers between devices  89.3 us (34%)
  blocking collectives  67.1 us (25%)
  Pallas kernels  39.6 us (15%)
  starting transfers between devices  23.7 us (9%)
  other arithmetic  20.7 us (8%)
  between operations  14 us (5%)
  local copies, waits for them, and re-layouts  9.21 us (3%)
    all_to_all x2, waiting for transfers between devices, summed(): terms = lax.all_to_all(part, axis, split_axis=0, concat_axis=0, tiled=True)  63.1 us
    all_to_all x1, blocking collectives, summed(): terms = lax.all_to_all(part, axis, split_axis=0, concat_axis=0, tiled=True)  51.7 us
    all_to_all x2, waiting for transfers between devices, entering(): every = lax.all_to_all(sent, 'ctx', split_axis=0, concat_axis=0, tiled=True)  16.5 us
    all_to_all x1, blocking collectives, entering(): lax.all_to_all(jnp.stack(found), 'ctx', split_axis=0, concat_axis=0, tile...  15.4 us
    pallas_call x1, Pallas kernels, on_device(): pl.pallas_call(middle_kernel, grid=(groups,), in_specs=[wide, wide, narro...  14.6 us
    pallas_call x1, Pallas kernels, on_device(): pl.pallas_call(forward_kernel, grid=(groups,), in_specs=[wide, wide, narr...  11.2 us
    all_to_all x2, starting transfers between devices, entering(): every = lax.all_to_all(sent, 'ctx', split_axis=0, concat_axis=0, tiled=True)  10.9 us
    pallas_call x1, Pallas kernels, on_device(): pl.pallas_call(backward_kernel, grid=(groups,), in_specs=[wide, wide, wid...  10.7 us
  transfers between devices with their start and end apart: 8, of which 6 were waited for; matrix products, arithmetic and copies ran while one was open for 6% of the time, Pallas kernels for 10%

profile of v1, /device:TPU:0, one launch (start us, length us, event | category | flops | bytes accessed | tf_op | source)
XLA Modules:
  0.0 263.6 jit_solution(14667789980483643479)
XLA Ops:
  7.2 0.0 copy-start
  7.2 1.2 copy-done
  8.4 0.0 copy-start.2
  8.4 0.9 copy-done.2
  9.4 0.0 copy-start.4
  9.4 0.8 copy-done.4
  10.1 3.1 %local_state.1 = (bf16[2,128,512]{2,1,0:T(8,128)(2,1)S(1)}, bf16[2,8,512]{2,1,0:T(8,128)(2,1)S(1)}) custom-call(bf16[512,1024]{1,0:T(8,128)(2,1)S(1)} %copy-done, bf16[512,256]{1,0:T(8,128)(2,1)S(1)} %copy-done.2, f32[16,512]{1,0:T(8,128)S(1)} %copy-done.4), custom_call_target="tpu_custom_call" | custom-call | flops 134217728 | bytes 1572864 | tf_op jit(solution)/shard_map/local_state/pallas_call | solution.py:310
  13.3 0.0 copy-start.9
  13.3 0.8 pad_maximum_fusion
  14.1 0.0 copy-start.3
  14.1 7.4 %all-to-all-start = ((bf16[8,2,24,512]{3,2,1,0:T(8,128)(2,1)}), bf16[8,2,24,512]{3,2,1,0:T(8,128)(2,1)S(1)}, u32[]{:S(2)}, u32[]{:S(2)}) async-start(bf16[8,2,24,512]{3,2,1,0:T(8,128)(2,1)} %pad_maximum_fusion), calls=%async_computation | async-start | bytes 786432 | tf_op jit(solution)/shard_map/all_to_all | solution.py:264
  21.5 0.0 all-gather.4.cloned.1.call-start
  21.6 0.7 all-gather.4.cloned.1.call-update
  22.3 0.6 constant_dynamic-update-slice_fusion.7
  22.9 10.3 %all-to-all-done = bf16[8,2,24,512]{3,2,1,0:T(8,128)(2,1)S(1)} async-done(((bf16[8,2,24,512]{3,2,1,0:T(8,128)(2,1)}), bf16[8,2,24,512]{3,2,1,0:T(8,128)(2,1)S(1)}, u32[]{:S(2)}, u32[]{:S(2)}) %all-to-all-start) | async-done | bytes 393248 | tf_op jit(solution)/shard_map/all_to_all | solution.py:264
  33.4 0.6 constant_dynamic-update-slice_fusion.6
  34.0 0.6 constant_dynamic-update-slice_fusion.5
  34.6 0.6 constant_dynamic-update-slice_fusion.4
  35.3 0.6 constant_dynamic-update-slice_fusion.3
  35.9 0.7 constant_dynamic-update-slice_fusion.2
  36.6 0.6 constant_dynamic-update-slice_fusion.1
  37.2 0.6 constant_dynamic-update-slice_fusion
  37.8 3.6 %all-to-all-start.1 = ((bf16[8,2,16,512]{3,2,1,0:T(8,128)(2,1)}), bf16[8,2,16,512]{3,2,1,0:T(8,128)(2,1)S(1)}, u32[]{:S(2)}, u32[]{:S(2)}) async-start(bf16[8,2,16,512]{3,2,1,0:T(8,128)(2,1)} %constant_dynamic-update-slice_fusion), calls=%async_computation.1 | async-start | bytes 524288 | tf_op jit(solution)/shard_map/all_to_all | solution.py:273
  41.4 0.0 copy-done.9
  41.4 0.1 broadcast_in_dim.6
  41.5 0.1 reshape_reshape.3.skip_ref
  41.6 8.6 %all-to-all-done.1 = bf16[8,2,16,512]{3,2,1,0:T(8,128)(2,1)S(1)} async-done(((bf16[8,2,16,512]{3,2,1,0:T(8,128)(2,1)}), bf16[8,2,16,512]{3,2,1,0:T(8,128)(2,1)S(1)}, u32[]{:S(2)}, u32[]{:S(2)}) %all-to-all-start.1) | async-done | bytes 262176 | tf_op jit(solution)/shard_map/all_to_all | solution.py:273
  50.2 0.0 all-gather.4.cloned.1.call-done.rows_ref
  50.3 0.0 copy-done.3
  50.3 0.0 copy-done.5
  50.3 0.0 copy-done.6
  50.3 0.0 copy-done.7
  50.3 11.2 %forward.1 = (f32[512,1024]{1,0:T(8,128)}, bf16[2,2,128,512]{3,2,1,0:T(8,128)(2,1)S(1)}, bf16[512,1024]{1,0:T(8,128)(2,1)}, bf16[1024,2048]{1,0:T(8,128)(2,1)}) custom-call(bf16[512,1024]{1,0:T(8,128)(2,1)} %x_ref.7, bf16[512,1024]{1,0:T(8,128)(2,1)} %z_ref.3, bf16[512,256]{1,0:T(8,128)(2,1)S(1)} %copy-done.3, bf16[512,256]{1,0:T(8,128)(2,1)S(1)} %copy-done.6, ...), custom_call_target="tpu_custom_call" | custom-call | flops 2147483648 | bytes 6291456 | tf_op jit(solution)/shard_map/forward/pallas_call | solution.py:322
  61.5 4.1 %fusion.8 = (bf16[512,2048]{1,0:T(8,128)(2,1)}, bf16[512,2048]{1,0:T(8,128)(2,1)S(1)}) fusion(bf16[1024,2048]{1,0:T(8,128)(2,1)} %get-tuple-element.38), kind=kLoop, calls=%fused_computation.57 | loop fusion | bytes 8388608 | tf_op jit(solution)/shard_map/slice | solution.py:340
  65.6 51.7 %all_to_all.47 = bf16[8,64,2048]{2,1,0:T(8,128)(2,1)} all-to-all(bf16[8,64,2048]{2,1,0:T(8,128)(2,1)S(1)} %bitcast.42), channel_id=1, replica_groups=mesh['ctx'=8,'head'=4] {'ctx'}, dimensions={0} | all-to-all | bytes 4194304 | tf_op jit(solution)/shard_map/all_to_all | solution.py:280
  117.3 4.4 %all-to-all-start.5 = ((bf16[8,64,2048]{2,1,0:T(8,128)(2,1)}), bf16[8,64,2048]{2,1,0:T(8,128)(2,1)}, u32[]{:S(2)}, u32[]{:S(2)}) async-start(bf16[8,64,2048]{2,1,0:T(8,128)(2,1)} %bitcast.10), calls=%async_computation.5 | async-start | bytes 4194304 | tf_op jit(solution)/shard_map/all_to_all | solution.py:280
  121.7 0.0 copy-start.1
  121.7 0.0 all-gather.8.cloned.1.call-start
  121.8 2.8 %reduce_sum.77 = bf16[64,2048]{1,0:T(8,128)(2,1)} reduce(bf16[8,64,2048]{2,1,0:T(8,128)(2,1)} %all_to_all.47, bf16[]{:T(256)} %constant.6.clone.1), dimensions={0}, to_apply=%region_6.7 | reduce | flops 917504 | bytes 2359298 | tf_op jit(solution)/shard_map/reduce_sum | solution.py:282
  124.5 0.0 all-gather.8.cloned.1.call-update
  124.6 0.0 copy-done.1
  124.6 14.6 %middle.1 = (bf16[512,2048]{1,0:T(8,128)(2,1)}, f32[512,1024]{1,0:T(8,128)}, f32[512,1024]{1,0:T(8,128)}, bf16[2,128,512]{2,1,0:T(8,128)(2,1)S(1)}, bf16[2,8,512]{2,1,0:T(8,128)(2,1)S(1)}) custom-call(bf16[512,1024]{1,0:T(8,128)(2,1)S(1)} %copy-done.1, bf16[512,1024]{1,0:T(8,128)(2,1)} %z_ref.3, bf16[512,256]{1,0:T(8,128)(2,1)S(1)} %copy-done.6, ...), custom_call_target="tpu_custom_call" | custom-call | flops 4294967296 | bytes 10485760 | tf_op jit(solution)/shard_map/middle/pallas_call | solution.py:344
  139.2 0.8 pad_maximum_fusion.1
  140.0 50.4 %all-to-all-done.5 = bf16[8,64,2048]{2,1,0:T(8,128)(2,1)} async-done(((bf16[8,64,2048]{2,1,0:T(8,128)(2,1)}), bf16[8,64,2048]{2,1,0:T(8,128)(2,1)}, u32[]{:S(2)}, u32[]{:S(2)}) %all-to-all-start.5) | async-done | bytes 2097184 | tf_op jit(solution)/shard_map/all_to_all | solution.py:280
  190.4 3.5 %all-to-all-start.3 = ((bf16[8,2,24,512]{3,2,1,0:T(8,128)(2,1)}), bf16[8,2,24,512]{3,2,1,0:T(8,128)(2,1)S(1)}, u32[]{:S(2)}, u32[]{:S(2)}) async-start(bf16[8,2,24,512]{3,2,1,0:T(8,128)(2,1)} %pad_maximum_fusion.1), calls=%async_computation.3 | async-start | bytes 786432 | tf_op jit(solution)/shard_map/all_to_all | solution.py:264
  193.9 0.2 all-gather.6.cloned.1.call-start
  194.1 2.7 %reduce_sum.76 = bf16[64,2048]{1,0:T(8,128)(2,1)} reduce(bf16[8,64,2048]{2,1,0:T(8,128)(2,1)} %all-to-all-done.5, bf16[]{:T(256)} %constant.6.clone.1), dimensions={0}, to_apply=%region_5.0 | reduce | flops 917504 | bytes 2359298 | tf_op jit(solution)/shard_map/reduce_sum | solution.py:282
  196.8 0.0 all-gather.6.cloned.1.call-update
  196.8 6.1 %all-to-all-done.3 = bf16[8,2,24,512]{3,2,1,0:T(8,128)(2,1)S(1)} async-done(((bf16[8,2,24,512]{3,2,1,0:T(8,128)(2,1)}), bf16[8,2,24,512]{3,2,1,0:T(8,128)(2,1)S(1)}, u32[]{:S(2)}, u32[]{:S(2)}) %all-to-all-start.3) | async-done | bytes 393248 | tf_op jit(solution)/shard_map/all_to_all | solution.py:264
  203.0 0.1 constant_dynamic-update-slice_fusion.15
  203.2 15.4 %all_to_all.48 = bf16[8,2,16,512]{3,2,1,0:T(8,128)(2,1)S(1)} all-to-all(bf16[8,2,16,512]{3,2,1,0:T(8,128)(2,1)S(1)} %constant_dynamic-update-slice_fusion.8), channel_id=1, replica_groups=mesh['ctx'=8,'head'=4] {'ctx'}, dimensions={0} | all-to-all | bytes 524288 | tf_op jit(solution)/shard_map/all_to_all | solution.py:273
  218.6 0.0 copy-done.8
  218.6 4.5 %all-to-all-start.2 = ((bf16[4,128,2048]{2,1,0:T(8,128)(2,1)}), bf16[4,128,2048]{2,1,0:T(8,128)(2,1)S(1)}, u32[]{:S(2)}, u32[]{:S(2)}) async-start(bf16[4,128,2048]{2,1,0:T(8,128)(2,1)} %bitcast.43), calls=%async_computation.2 | async-start | bytes 4194304 | tf_op jit(solution)/shard_map/all_to_all | solution.py:280
  223.1 0.9 slice_convert_fusion
  224.1 0.1 slice_reduce_fusion
  224.1 0.6 copy.52
  224.7 0.1 reduce_sum.73
  224.8 0.1 reduce_sum.74
  224.9 0.6 reshape.88
  225.5 10.7 %backward.1 = (f32[512,1024]{1,0:T(8,128)}, f32[512,256]{1,0:T(8,128)}, f32[512,256]{1,0:T(8,128)}, f32[16,512]{1,0:T(8,128)}) custom-call(bf16[512,1024]{1,0:T(8,128)(2,1)} %x_ref.7, f32[512,1024]{1,0:T(8,128)} %get-tuple-element.29.dy_ref, f32[512,1024]{1,0:T(8,128)} %get-tuple-element.26.core_ref, bf16[512,256]{1,0:T(8,128)(2,1)S(1)} %copy-done.3, ...), custom_call_target="tpu_custom_call" | custom-call | flops 4294967296 | bytes 8388608 | tf_op jit(solution)/shard_map/backward/pallas_call | solution.py:364
  236.2 12.6 %all-to-all-done.2 = bf16[4,128,2048]{2,1,0:T(8,128)(2,1)S(1)} async-done(((bf16[4,128,2048]{2,1,0:T(8,128)(2,1)}), bf16[4,128,2048]{2,1,0:T(8,128)(2,1)S(1)}, u32[]{:S(2)}, u32[]{:S(2)}) %all-to-all-start.2) | async-done | bytes 2097184 | tf_op jit(solution)/shard_map/all_to_all | solution.py:280
  248.8 1.3 reduce_sum.71
  250.1 0.4 all-gather.6.cloned.1.call-done
  250.5 6.5 %maximum_convert_fusion = f32[1024,2048]{1,0:T(8,128)} fusion(bf16[512,2048]{1,0:T(8,128)(2,1)} %all-gather.8.cloned.1.call-done, bf16[512,2048]{1,0:T(8,128)(2,1)} %all-gather.6.cloned.1.call-done), kind=kLoop, calls=%fused_computation | loop fusion | flops 8388608 | bytes 12582912 | tf_op jit(solution)/shard_map/concatenate | solution.py:342
  (26 shorter events, 0.3 us)
Async XLA Ops:
  7.2 1.2 copy-start
  8.4 0.9 copy-start.2
  9.4 0.8 copy-start.4
  13.3 28.1 %copy-start.9 = (f32[16]{0:T(128)S(1)}, f32[16]{0:T(128)}, u32[]{:S(2)}) copy-start(f32[16]{0:T(128)} %param.14) | copy-start | bytes 196
  14.1 36.2 %copy-start.3 = (bf16[512,256]{1,0:T(8,128)(2,1)S(1)}, bf16[512,256]{1,0:T(8,128)(2,1)}, u32[]{:S(2)}) copy-start(bf16[512,256]{1,0:T(8,128)(2,1)} %b_ref.5) | copy-start | bytes 786436
  14.1 36.2 %copy-start.5 = (f32[16,512]{1,0:T(8,128)S(1)}, f32[16,512]{1,0:T(8,128)}, u32[]{:S(2)}) copy-start(f32[16,512]{1,0:T(8,128)} %log_ref.7) | copy-start | bytes 98308
  14.1 36.2 %copy-start.6 = (bf16[512,256]{1,0:T(8,128)(2,1)S(1)}, bf16[512,256]{1,0:T(8,128)(2,1)}, u32[]{:S(2)}) copy-start(bf16[512,256]{1,0:T(8,128)(2,1)} %c_ref.5) | copy-start | bytes 786436
  14.1 36.2 %copy-start.7 = (f32[1024]{0:T(1024)S(1)}, f32[1024]{0:T(1024)}, u32[]{:S(2)}) copy-start(f32[1024]{0:T(1024)} %param.15) | copy-start | bytes 12292
  14.1 19.1 %all-to-all-start = ((bf16[8,2,24,512]{3,2,1,0:T(8,128)(2,1)}), bf16[8,2,24,512]{3,2,1,0:T(8,128)(2,1)S(1)}, u32[]{:S(2)}, u32[]{:S(2)}) async-start(bf16[8,2,24,512]{3,2,1,0:T(8,128)(2,1)} %pad_maximum_fusion), calls=%async_computation | async-start | bytes 786432 | tf_op jit(solution)/shard_map/all_to_all | solution.py:264
  21.5 28.7 %all-gather.4.cloned.1.call-start = ((), (), s32[]{:S(2)}) async-start(), calls=%async_computation.7 | async-start | bytes 2621440 | tf_op jit(solution)/shard_map/all_gather | solution.py:308
  37.8 12.4 %all-to-all-start.1 = ((bf16[8,2,16,512]{3,2,1,0:T(8,128)(2,1)}), bf16[8,2,16,512]{3,2,1,0:T(8,128)(2,1)S(1)}, u32[]{:S(2)}, u32[]{:S(2)}) async-start(bf16[8,2,16,512]{3,2,1,0:T(8,128)(2,1)} %constant_dynamic-update-slice_fusion), calls=%async_computation.1 | async-start | bytes 524288 | tf_op jit(solution)/shard_map/all_to_all | solution.py:273
  117.3 73.1 %all-to-all-start.5 = ((bf16[8,64,2048]{2,1,0:T(8,128)(2,1)}), bf16[8,64,2048]{2,1,0:T(8,128)(2,1)}, u32[]{:S(2)}, u32[]{:S(2)}) async-start(bf16[8,64,2048]{2,1,0:T(8,128)(2,1)} %bitcast.10), calls=%async_computation.5 | async-start | bytes 4194304 | tf_op jit(solution)/shard_map/all_to_all | solution.py:280
  121.7 2.9 %copy-start.1 = (bf16[512,1024]{1,0:T(8,128)(2,1)S(1)}, bf16[512,1024]{1,0:T(8,128)(2,1)}, u32[]{:S(2)}) copy-start(bf16[512,1024]{1,0:T(8,128)(2,1)} %x_ref.7) | copy-start | bytes 3145732
  121.7 128.4 %all-gather.8.cloned.1.call-start = ((), (), s32[]{:S(2)}) async-start(), calls=%async_computation.9 | async-start | bytes 2359296 | tf_op jit(solution)/shard_map/all_gather | solution.py:341
  190.4 12.6 %all-to-all-start.3 = ((bf16[8,2,24,512]{3,2,1,0:T(8,128)(2,1)}), bf16[8,2,24,512]{3,2,1,0:T(8,128)(2,1)S(1)}, u32[]{:S(2)}, u32[]{:S(2)}) async-start(bf16[8,2,24,512]{3,2,1,0:T(8,128)(2,1)} %pad_maximum_fusion.1), calls=%async_computation.3 | async-start | bytes 786432 | tf_op jit(solution)/shard_map/all_to_all | solution.py:264
  193.9 56.7 %all-gather.6.cloned.1.call-start = ((), (), s32[]{:S(2)}) async-start(), calls=%async_computation.8 | async-start | bytes 2359296 | tf_op jit(solution)/shard_map/all_gather | solution.py:341
  203.0 15.6 %copy-start.8 = (bf16[8,2,24,512]{3,2,1,0:T(8,128)(2,1)}, bf16[8,2,24,512]{3,2,1,0:T(8,128)(2,1)S(1)}, u32[]{:S(2)}) copy-start(bf16[8,2,24,512]{3,2,1,0:T(8,128)(2,1)S(1)} %all-to-all-done.3) | copy-start | bytes 1179652
  218.6 30.2 %all-to-all-start.2 = ((bf16[4,128,2048]{2,1,0:T(8,128)(2,1)}), bf16[4,128,2048]{2,1,0:T(8,128)(2,1)S(1)}, u32[]{:S(2)}, u32[]{:S(2)}) async-start(bf16[4,128,2048]{2,1,0:T(8,128)(2,1)} %bitcast.43), calls=%async_computation.2 | async-start | bytes 4194304 | tf_op jit(solution)/shard_map/all_to_all | solution.py:280
Sparse Core Ops, SparseCore 0:
  23.9 23.9 all-gather.3
  124.7 70.4 all-gather.7
  197.3 53.1 all-gather.5
